TPU v7x, 32 devices: a whole 2x2x4 slice. The times are simulated.
32 devices in a mesh: row: 2 (over x), col: 4 (over z), box: 4 (over y, core).
Axes of the slice: x: 2, y: 2, z: 4, core: 2. Of those that a mesh axis runs over, the one named last changes fastest.
Arguments:
- coeffs: bfloat16 [81920, 512], P(('row', 'box'), 'col'), may hold values from -6 to 6
- reflectors: bfloat16 [81920, 256], P(('row', 'box')), may hold values from -0.078125 to 0.078125
- factor: float32 [256, 256], replicated, may hold values from -0.375 to 0.375
- func_exp: float32 [81920], replicated, may hold values from 0.5 to 20
- func_atom: int32 [81920], replicated, may hold values from 0 to 8191, never falling along the last dimension, each value on 1 to 20 neighbouring positions
- atom_pos: float32 [3, 8192], replicated, may hold values from 0 to 1
- point_pos: float32 [3, 128, 128], P(None, ('row', 'col', 'box')), may hold values from 0 to 1
- send_tiles: int32 [8, 8, 2], replicated, may hold values from 0 to 79, as said below
- box_tiles: int32 [128, 16], P(('row', 'col', 'box')), may hold values from 0 to 15, as said below
- box_count: int32 [128], P(('row', 'col', 'box')), may hold values from 1 to 16
Outputs:
- rotated: bfloat16 [81920, 512], P(('row', 'box'), 'col')
- density: float32 [128, 128], P(('row', 'col', 'box'))
Inputs may be any that keep to these rules, and one draw needn't show every extreme that they name: `send_tiles`: for each basis group and box group the 2 tiles are different local tiles of the basis group. `box_tiles`: the 16 slots listed by a box are different. `func_atom`: never falls along the basis functions; every atom carries 1 to 20 functions.
All inputs are finite; a program needn't handle non-finite values.
Results may differ from a plain program's by a relative error of at most 0.015.
Values may be sent and summed in bfloat16 or wider, within the bound.
A program may use at most 128 MiB of HBM per device.

v0:
```python
import math
import jax
import jax.numpy as jnp
from jax import lax
from jax.sharding import PartitionSpec as P

K = 512
TILE = 128


def box_density(arrived, slot_alpha, slot_centre, listed, count, points):
    alpha = slot_alpha[listed]
    centre = slot_centre[:, listed]
    first = points[0][:, None, None] - centre[0][None]
    dist = first * first
    second = points[1][:, None, None] - centre[1][None]
    dist = dist + second * second
    third = points[2][:, None, None] - centre[2][None]
    dist = dist + third * third
    live = jnp.arange(listed.shape[0], dtype=jnp.int32) < count
    phi = jnp.where(live[None, :, None], jnp.exp(-alpha[None] * dist), 0.0).astype(jnp.bfloat16)
    phi = phi.reshape(points.shape[1], -1)
    block = arrived[listed].reshape(-1, arrived.shape[2])
    orbital = jnp.dot(phi, block, preferred_element_type=jnp.float32)
    return jnp.sum(orbital * orbital, 1) / (K * TILE)


def by_blocks(arrived, slot_alpha, slot_centre, lists, counts, points):
    boxes = lists.shape[0]
    width = math.gcd(boxes, 2)
    steps = boxes // width
    lists_blocked = lists.reshape(steps, width, lists.shape[1])
    counts_blocked = counts.reshape(steps, width)
    moved = jnp.moveaxis(points, 1, 0)
    points_blocked = moved.reshape(steps, width, moved.shape[1], moved.shape[2])
    single = jax.vmap(
        lambda listed, count, where: box_density(
            arrived, slot_alpha, slot_centre, listed, count, where
        )
    )

    def one_block(items):
        return single(items[0], items[1], items[2])

    result = lax.map(one_block, (lists_blocked, counts_blocked, points_blocked))
    return result.reshape(boxes, result.shape[2])


def per_device(
    coeffs,
    reflectors,
    factor,
    func_exp,
    func_atom,
    atom_pos,
    point_pos,
    send_tiles,
    box_tiles,
    box_count,
):
    panel_part = jnp.dot(reflectors.T, coeffs, preferred_element_type=jnp.float32)
    panel = lax.psum(panel_part.astype(jnp.bfloat16), ("row", "box")).astype(jnp.float32)
    scaled = jnp.dot(factor, panel, precision=lax.Precision.HIGHEST).astype(jnp.bfloat16)
    rotated = (
        coeffs.astype(jnp.float32) - jnp.dot(reflectors, scaled, preferred_element_type=jnp.float32)
    ).astype(jnp.bfloat16)
    peers = lax.axis_size(("row", "box"))
    group = lax.axis_index(("row", "box"))
    capacity = send_tiles.shape[2]
    local_tiles = coeffs.shape[0] // TILE
    slots = jnp.arange(peers * capacity, dtype=jnp.int32)
    source = slots // capacity
    within = slots % capacity
    tile = source * local_tiles + send_tiles[source, group, within]
    funcs = tile[:, None] * TILE + jnp.arange(TILE, dtype=jnp.int32)[None, :]
    slot_alpha = func_exp[funcs]
    slot_centre = atom_pos[:, func_atom[funcs]]
    outgoing_index = send_tiles[group]
    outgoing = rotated.reshape(local_tiles, TILE, rotated.shape[1])[outgoing_index]
    arrived = lax.all_to_all(outgoing, ("row", "box"), split_axis=0, concat_axis=0, tiled=True)
    arrived = arrived.reshape(peers * capacity, TILE, arrived.shape[3])
    lists, counts = (
        lax.all_gather(box_tiles, "col", axis=0, tiled=True),
        lax.all_gather(box_count, "col", axis=0, tiled=True),
    )
    points = lax.all_gather(point_pos, "col", axis=1, tiled=True)
    partial_value = by_blocks(arrived, slot_alpha, slot_centre, lists, counts, points)
    density = lax.psum_scatter(
        partial_value.astype(jnp.bfloat16), "col", scatter_dimension=0, tiled=True
    ).astype(jnp.float32)
    return (rotated, density)


def solution(mesh):
    in_specs = (
        P(("row", "box"), "col"),
        P(("row", "box"), None),
        P(),
        P(),
        P(),
        P(),
        P(None, ("row", "col", "box"), None),
        P(),
        P(("row", "col", "box"), None),
        P(("row", "col", "box")),
    )
    out_specs = (P(("row", "box"), "col"), P(("row", "col", "box"), None))
    return jax.shard_map(
        per_device, mesh=mesh, in_specs=in_specs, out_specs=out_specs, check_vma=False
    )
```

profile of v0, /device:TPU:0, one launch (start us, length us, event | category | flops | bytes accessed | tf_op | source)
XLA Modules:
  0.0 196.5 jit_solution(6431484893824231304)
XLA Ops:
  7.2 5.5 %convolution_convert_fusion = bf16[256,128]{1,0:T(8,128)(2,1)} fusion(bf16[10240,256]{1,0:T(8,128)(2,1)} %param.13, bf16[10240,128]{1,0:T(8,128)(2,1)} %param.12), kind=kOutput, calls=%fused_computation.42 | convolution fusion | flops 671121408 | bytes 7929856 | tf_op jit(solution)/shard_map/dot_general | solution.py:61
  12.9 0.7 gather_fusion.3
  13.8 3.0 %copy.28 = bf16[10240,128]{0,1:T(8,128)(2,1)S(1)} copy(bf16[10240,128]{1,0:T(8,128)(2,1)} %param.12) | data formatting | bytes 5242880 | tf_op args[0]
  16.8 2.6 %copy.31 = f32[3,8192]{0,1:T(8,128)} copy(f32[3,8192]{1,0:T(4,128)S(1)} %copy-done.5) | data formatting | bytes 196608 | tf_op args[5]
  19.4 48.7 %all-reduce.4.cloned.1.call-done = bf16[256,128]{1,0:T(8,128)(2,1)} async-done(((bf16[256,128]{1,0:T(8,128)(2,1)}), bf16[256,128]{1,0:T(8,128)(2,1)}) %all-reduce.4.cloned.1.call-update) | async-done | bytes 65552 | tf_op jit(solution)/shard_map/psum | solution.py:62
  68.1 1.1 convolution_convert_fusion.1
  69.3 5.8 %fusion.13 = bf16[10240,128]{0,1:T(8,128)(2,1)} fusion(bf16[128,256]{1,0:T(8,128)(2,1)S(1)} %convolution_convert_fusion.1, bf16[10240,256]{1,0:T(8,128)(2,1)} %param.13, bf16[10240,128]{0,1:T(8,128)(2,1)S(1)} %copy.28), kind=kOutput, calls=%fused_computation.41 | convolution fusion | flops 675020800 | bytes 10551296 | tf_op jit(solution)/shard_map/dot_general | solution.py:65
  75.1 3.2 %copy.36 = bf16[10240,128]{1,0:T(8,128)(2,1)S(1)} copy(bf16[10240,128]{0,1:T(8,128)(2,1)} %fusion.13) | data formatting | bytes 5242880
  78.3 1.6 gather_fusion.7
  80.0 3.5 %all-to-all-start = ((bf16[8,2,128,128]{3,2,1,0:T(8,128)(2,1)}), bf16[8,2,128,128]{3,2,1,0:T(8,128)(2,1)S(1)}, u32[]{:S(2)}, u32[]{:S(2)}) async-start(bf16[8,2,128,128]{3,2,1,0:T(8,128)(2,1)} %bitcast.116), calls=%async_computation | async-start | bytes 1048576 | tf_op jit(solution)/shard_map/all_to_all | solution.py:80
  83.6 11.8 %gather_fusion.5 = s32[2048]{0:T(1024)S(1)} fusion(s32[81920]{0:T(1024)S(1)} %copy-done, s32[2048]{0:T(1024)S(1)} %fusion.15), kind=kCustom, calls=%fused_computation.5 | custom fusion | bytes 24576 | tf_op jit(solution)/shard_map/gather | solution.py:77
  95.4 7.7 %gather_fusion.6 = f32[2048,3]{1,0:T(8,128)S(1)} fusion(f32[3,8192]{0,1:T(8,128)} %copy.31, s32[2048]{0:T(1024)S(1)} %fusion.17), kind=kCustom, calls=%fused_computation.6 | custom fusion | bytes 57344 | tf_op jit(solution)/shard_map/gather | solution.py:77
  103.4 11.8 %gather_fusion.4 = f32[2048]{0:T(1024)S(1)} fusion(f32[81920]{0:T(1024)S(1)} %copy-done.1, s32[2048]{0:T(1024)S(1)} %fusion.15), kind=kCustom, calls=%fused_computation.4 | custom fusion | bytes 24576 | tf_op jit(solution)/shard_map/gather | solution.py:76
  115.3 0.7 fusion.28
  116.8 8.3 %all-reduce = s32[16]{0:T(128)S(1)} all-reduce(s32[16]{0:T(128)S(1)} %dynamic-update-slice), channel_id=1, replica_groups=mesh['row'=2,'col'=4,'box'=4] {'col'}, use_global_device_ids=true, to_apply=%add | all-reduce | flops 16 | bytes 128
  125.1 13.1 %all_gather.11 = f32[3,16,128]{2,0,1:T(4,128)S(1)} all-gather(f32[3,4,128]{2,0,1:T(4,128)S(1)} %copy.29), channel_id=1, replica_groups=mesh['row'=2,'col'=4,'box'=4] {'col'}, dimensions={1}, use_global_device_ids=true | all-gather | bytes 30720 | tf_op jit(solution)/shard_map/all_gather | solution.py:86
  138.9 11.9 %all-gather = s32[4,4,16]{2,1,0:T(4,128)S(1)} all-gather(s32[1,4,16]{2,1,0:T(4,128)S(1)} %bitcast.126), channel_id=1, replica_groups=mesh['row'=2,'col'=4,'box'=4] {'col'}, dimensions={0}, use_global_device_ids=true | all-gather | bytes 1280 | tf_op jit(solution)/shard_map/all_gather | solution.py:83
  150.8 29.7 %while.10 = (s32[]{:T(128)}, bf16[8,2,128]{2,1,0:T(2,128)(2,1)S(1)}, s32[8,2]{1,0:T(8,128)S(1)}, s32[8,2,16]{2,1,0:T(2,128)S(1)}, f32[16,128]{1,0:T(8,128)S(1)},...) while((s32[]{:T(128)}, ...), condition=%wide.region_3.4_spmd, body=%wide.region_1.3_spmd.sunk | while | flops 140055680 | bytes 3644613 | solution.py:45
  150.9 0.6 gather_fusion.1
  151.7 0.7 gather_fusion
  152.5 0.6 gather_fusion.2
  153.3 1.2 fusion.41
  154.6 0.6 gather_fusion.1
  155.4 0.7 gather_fusion
  156.2 0.6 gather_fusion.2
  157.0 1.2 fusion.41
  158.3 0.6 gather_fusion.1
  159.1 0.7 gather_fusion
  160.7 1.2 fusion.41
  162.1 0.6 gather_fusion.1
  162.8 0.7 gather_fusion
  163.6 0.6 gather_fusion.2
  164.4 1.2 fusion.41
  165.8 0.6 gather_fusion.1
  166.5 0.7 gather_fusion
  167.3 0.6 gather_fusion.2
  168.1 1.2 fusion.41
  169.5 0.6 gather_fusion.1
  170.3 0.7 gather_fusion
  171.8 1.2 fusion.41
  173.2 0.6 gather_fusion.1
  174.0 0.7 gather_fusion
  175.5 1.2 fusion.41
  176.9 0.6 gather_fusion.1
  177.7 0.7 gather_fusion
  179.3 1.2 fusion.41
  180.5 8.6 %all-reduce.1 = bf16[16,128]{1,0:T(8,128)(2,1)S(1)} all-reduce(bf16[16,128]{1,0:T(8,128)(2,1)S(1)} %bitcast.125), channel_id=2, replica_groups=mesh['row'=2,'col'=4,'box'=4] {'col'}, use_global_device_ids=true, to_apply=%region_4.5.clone | all-reduce | flops 2048 | bytes 8192
  189.1 0.6 dynamic-slice_convert_fusion
  (162 shorter events, 7.2 us)
Async XLA Ops:
  7.2 76.4 %copy-start = (s32[81920]{0:T(1024)S(1)}, s32[81920]{0:T(1024)}, u32[]{:S(2)}) copy-start(s32[81920]{0:T(1024)} %param.16) | copy-start | bytes 983044
  7.2 5.7 %copy-start.2 = (s32[8,8,2]{1,2,0:T(2,128)S(1)}, s32[8,8,2]{1,2,0:T(2,128)}, u32[]{:S(2)}) copy-start(s32[8,8,2]{1,2,0:T(2,128)} %param.19) | copy-start | bytes 1540
  7.2 60.9 %all-reduce.4.cloned.1.call-start = ((), (), s32[]{:S(2)}) async-start(), calls=%async_computation.1 | async-start | bytes 131072 | tf_op jit(solution)/shard_map/psum | solution.py:62
  13.7 3.1 %copy-start.5 = (f32[3,8192]{1,0:T(4,128)S(1)}, f32[3,8192]{1,0:T(4,128)}, u32[]{:S(2)}) copy-start(f32[3,8192]{1,0:T(4,128)} %param.17) | copy-start | bytes 294916
  16.8 51.3 %copy-start.4 = (f32[256,256]{1,0:T(8,128)S(1)}, f32[256,256]{1,0:T(8,128)}, u32[]{:S(2)}) copy-start(f32[256,256]{1,0:T(8,128)} %param.14) | copy-start | bytes 786436
  78.3 5.2 %copy-start.3 = (bf16[10240,128]{1,0:T(8,128)(2,1)}, bf16[10240,128]{1,0:T(8,128)(2,1)S(1)}, u32[]{:S(2)}) copy-start(bf16[10240,128]{1,0:T(8,128)(2,1)S(1)} %copy.36) | copy-start | bytes 7864324
  80.0 70.8 %all-to-all-start = ((bf16[8,2,128,128]{3,2,1,0:T(8,128)(2,1)}), bf16[8,2,128,128]{3,2,1,0:T(8,128)(2,1)S(1)}, u32[]{:S(2)}, u32[]{:S(2)}) async-start(bf16[8,2,128,128]{3,2,1,0:T(8,128)(2,1)} %bitcast.116), calls=%async_computation | async-start | bytes 1048576 | tf_op jit(solution)/shard_map/all_to_all | solution.py:80
  95.4 8.1 %copy-start.1 = (f32[81920]{0:T(1024)S(1)}, f32[81920]{0:T(1024)}, u32[]{:S(2)}) copy-start(f32[81920]{0:T(1024)} %param.15) | copy-start | bytes 983044
  103.4 11.8 %copy-start.8 = (u32[32]{0:T(128)S(1)}, u32[32]{0:T(128)}, u32[]{:S(2)}) copy-start(u32[32]{0:T(128)} %constant.107) | copy-start | bytes 388
  103.4 13.1 %copy-start.9 = (s32[4]{0:T(128)S(1)}, s32[4]{0:T(128)}, u32[]{:S(2)}) copy-start(s32[4]{0:T(128)} %param.21) | copy-start | bytes 52
  103.4 21.7 %copy-start.6 = (f32[3,4,128]{2,1,0:T(4,128)S(1)}, f32[3,4,128]{2,1,0:T(4,128)}, u32[]{:S(2)}) copy-start(f32[3,4,128]{2,1,0:T(4,128)} %param.18) | copy-start | bytes 18436
  103.4 35.5 %copy-start.7 = (s32[4,16]{1,0:T(4,128)S(1)}, s32[4,16]{1,0:T(4,128)}, u32[]{:S(2)}) copy-start(s32[4,16]{1,0:T(4,128)} %param.20) | copy-start | bytes 772
Sparse Core Ops, SparseCore 0:
  12.9 55.1 all-reduce.3
where the time goes:
time: 197 us
  local copies, waits for them, and re-layouts  62.4 us (32%)
  waiting for transfers between devices  48.7 us (25%)
  blocking collectives  41.9 us (21%)
  matrix products  22.2 us (11%)
  between operations  15.6 us (8%)
  starting transfers between devices  3.53 us (2%)
    psum x1, waiting for transfers between devices, per_device(): lax.psum(panel_part.astype(jnp.bfloat16), ('row', 'box'))  48.7 us
    gather x3, local copies, waits for them, and re-layouts, per_device(): slot_centre = atom_pos[:, func_atom[funcs]]  19.8 us
    unnamed x2, blocking collectives  16.9 us
    all_gather x1, blocking collectives, per_device(): points = lax.all_gather(point_pos, 'col', axis=1, tiled=True)  13.1 us
    all_gather x1, blocking collectives, per_device(): lax.all_gather(box_tiles, 'col', axis=0, tiled=True)  11.9 us
    gather x1, local copies, waits for them, and re-layouts, per_device(): slot_alpha = func_exp[funcs]  11.8 us
    unnamed x27, local copies, waits for them, and re-layouts  9.83 us
    dot_general x8, matrix products, box_density(): orbital = jnp.dot(phi, block, preferred_element_type=jnp.float32)  9.66 us
  transfers between devices with their start and end apart: 2, of which 1 were waited for; matrix products, arithmetic and copies ran while one was open for 20% of the time, Pallas kernels for 0%

commit v1 on v0

--- a/solution.py
+++ b/solution.py
@@ -83,7 +83,16 @@
         lax.all_gather(box_tiles, "col", axis=0, tiled=True),
         lax.all_gather(box_count, "col", axis=0, tiled=True),
     )
-    points = lax.all_gather(point_pos, "col", axis=1, tiled=True)
+    ways = lax.axis_size("col")
+    up = [(d, (d + 1) % ways) for d in range(ways)]
+    down = [(d, (d - 1) % ways) for d in range(ways)]
+    earlier, later = ([point_pos], [point_pos])
+    for _ in range(ways // 2):
+        earlier.append(lax.ppermute(earlier[-1], "col", up))
+    for _ in range((ways - 1) // 2):
+        later.append(lax.ppermute(later[-1], "col", down))
+    line = jnp.concatenate([*earlier[::-1], *later[1:]], axis=1)
+    points = jnp.roll(line, (lax.axis_index("col") - ways // 2) * point_pos.shape[1], axis=1)
     partial_value = by_blocks(arrived, slot_alpha, slot_centre, lists, counts, points)
     density = lax.psum_scatter(
         partial_value.astype(jnp.bfloat16), "col", scatter_dimension=0, tiled=True

time: 197 us -> 191 us (0.970)
  blocking collectives: 41.9 us -> 28.7 us
  starting transfers between devices: 3.53 us -> 10.2 us
    all_gather x1 -> x0, blocking collectives: 13.1 us -> none  [per_device(): points = lax.all_gather(point_pos, 'col', axis=1, tiled=True)]
    ppermute x0 -> x3, starting transfers between devices: none -> 6.71 us  [the longest x2 4.61 us: per_device(): earlier.append(lax.ppermute(earlier[-1], 'col', up))]
    unnamed x27 -> x24, local copies, waits for them, and re-layouts: 9.83 us -> 10.7 us
  transfers between devices with their start and end apart: 2 -> 5, of which waited for: 1 -> 1; matrix products, arithmetic and copies ran while one was open for 20% -> 30% of each run, Pallas kernels for 0% -> 0%
where the time goes in v1:
time: 191 us
  local copies, waits for them, and re-layouts  63.3 us (33%)
  waiting for transfers between devices  48.3 us (25%)
  blocking collectives  28.7 us (15%)
  matrix products  22.1 us (12%)
  between operations  15.6 us (8%)
  starting transfers between devices  10.2 us (5%)
    psum x1, waiting for transfers between devices, per_device(): lax.psum(panel_part.astype(jnp.bfloat16), ('row', 'box'))  48.2 us
    gather x3, local copies, waits for them, and re-layouts, per_device(): slot_centre = atom_pos[:, func_atom[funcs]]  19.8 us
    unnamed x2, blocking collectives  16.8 us
    all_gather x1, blocking collectives, per_device(): lax.all_gather(box_tiles, 'col', axis=0, tiled=True)  11.9 us
    gather x1, local copies, waits for them, and re-layouts, per_device(): slot_alpha = func_exp[funcs]  11.8 us
    unnamed x24, local copies, waits for them, and re-layouts  10.7 us
    dot_general x8, matrix products, box_density(): orbital = jnp.dot(phi, block, preferred_element_type=jnp.float32)  9.66 us
    gather x8, local copies, waits for them, and re-layouts, box_density(): block = arrived[listed].reshape(-1, arrived.shape[2])  5.99 us
  transfers between devices with their start and end apart: 5, of which 1 were waited for; matrix products, arithmetic and copies ran while one was open for 30% of the time, Pallas kernels for 0%

profile of v1, /device:TPU:0, one launch (start us, length us, event | category | flops | bytes accessed | tf_op | source)
XLA Modules:
  0.0 190.5 jit_solution(9481398206345519462)
XLA Ops:
  7.2 3.1 %collective-permute-start = (f32[3,4,128]{2,1,0:T(4,128)}, f32[3,4,128]{2,1,0:T(4,128)S(1)}, u32[]{:S(2)}, u32[]{:S(2)}) collective-permute-start(f32[3,4,128]{2,1,0:T(4,128)} %param.18), channel_id=1, source_target_pairs={{0,4},{4,8},{8,12},{12,0},{1,5},{5,9},{9,13},{13,1},{2,6},{6,10},{... | collective-permute-start | bytes 18440 | tf_op jit(solution)/shard_map/ppermute | solution.py:91
  10.3 2.1 %collective-permute-start.2 = (f32[3,4,128]{2,1,0:T(4,128)}, f32[3,4,128]{2,1,0:T(4,128)S(1)}, u32[]{:S(2)}, u32[]{:S(2)}) collective-permute-start(f32[3,4,128]{2,1,0:T(4,128)} %param.18), channel_id=1, source_target_pairs={{0,12},{4,0},{8,4},{12,8},{1,13},{5,1},{9,5},{13,9},{2,14},{6,2},{... | collective-permute-start | bytes 18440 | tf_op jit(solution)/shard_map/ppermute | solution.py:93
  12.4 5.5 %convolution_convert_fusion = bf16[256,128]{1,0:T(8,128)(2,1)} fusion(bf16[10240,256]{1,0:T(8,128)(2,1)} %param.13, bf16[10240,128]{1,0:T(8,128)(2,1)} %param.12), kind=kOutput, calls=%fused_computation.42 | convolution fusion | flops 671121408 | bytes 7929856 | tf_op jit(solution)/shard_map/dot_general | solution.py:61
  18.0 0.7 gather_fusion.3
  18.9 3.0 %copy.28 = bf16[10240,128]{0,1:T(8,128)(2,1)S(1)} copy(bf16[10240,128]{1,0:T(8,128)(2,1)} %param.12) | data formatting | bytes 5242880 | tf_op args[0]
  21.9 48.2 %all-reduce.4.cloned.1.call-done = bf16[256,128]{1,0:T(8,128)(2,1)} async-done(((bf16[256,128]{1,0:T(8,128)(2,1)}), bf16[256,128]{1,0:T(8,128)(2,1)}) %all-reduce.4.cloned.1.call-update) | async-done | bytes 65552 | tf_op jit(solution)/shard_map/psum | solution.py:62
  70.2 1.1 convolution_convert_fusion.1
  71.3 5.8 %fusion.13 = bf16[10240,128]{0,1:T(8,128)(2,1)} fusion(bf16[128,256]{1,0:T(8,128)(2,1)S(1)} %convolution_convert_fusion.1, bf16[10240,256]{1,0:T(8,128)(2,1)} %param.13, bf16[10240,128]{0,1:T(8,128)(2,1)S(1)} %copy.28), kind=kOutput, calls=%fused_computation.41 | convolution fusion | flops 675020800 | bytes 10551296 | tf_op jit(solution)/shard_map/dot_general | solution.py:65
  77.1 3.2 %copy.34 = bf16[10240,128]{1,0:T(8,128)(2,1)S(1)} copy(bf16[10240,128]{0,1:T(8,128)(2,1)} %fusion.13) | data formatting | bytes 5242880
  80.4 1.6 gather_fusion.7
  82.0 3.5 %all-to-all-start = ((bf16[8,2,128,128]{3,2,1,0:T(8,128)(2,1)}), bf16[8,2,128,128]{3,2,1,0:T(8,128)(2,1)S(1)}, u32[]{:S(2)}, u32[]{:S(2)}) async-start(bf16[8,2,128,128]{3,2,1,0:T(8,128)(2,1)} %bitcast.116), calls=%async_computation | async-start | bytes 1048576 | tf_op jit(solution)/shard_map/all_to_all | solution.py:80
  85.6 11.8 %gather_fusion.5 = s32[2048]{0:T(1024)S(1)} fusion(s32[81920]{0:T(1024)S(1)} %copy-done, s32[2048]{0:T(1024)S(1)} %fusion.15), kind=kCustom, calls=%fused_computation.5 | custom fusion | bytes 24576 | tf_op jit(solution)/shard_map/gather | solution.py:77
  97.4 1.5 collective-permute-start.1
  99.0 3.5 %copy.29 = f32[3,8192]{0,1:T(8,128)} copy(f32[3,8192]{1,0:T(4,128)} %param.17) | data formatting | bytes 196608 | tf_op args[5]
  102.5 7.6 %gather_fusion.6 = f32[2048,3]{1,0:T(8,128)S(1)} fusion(f32[3,8192]{0,1:T(8,128)} %copy.29, s32[2048]{0:T(1024)S(1)} %fusion.17), kind=kCustom, calls=%fused_computation.6 | custom fusion | bytes 57344 | tf_op jit(solution)/shard_map/gather | solution.py:77
  110.5 11.8 %gather_fusion.4 = f32[2048]{0:T(1024)S(1)} fusion(f32[81920]{0:T(1024)S(1)} %copy-done.1, s32[2048]{0:T(1024)S(1)} %fusion.15), kind=kCustom, calls=%fused_computation.4 | custom fusion | bytes 24576 | tf_op jit(solution)/shard_map/gather | solution.py:76
  122.3 0.7 fusion.28
  123.8 8.3 %all-reduce = s32[16]{0:T(128)S(1)} all-reduce(s32[16]{0:T(128)S(1)} %dynamic-update-slice), channel_id=1, replica_groups=mesh['row'=2,'col'=4,'box'=4] {'col'}, use_global_device_ids=true, to_apply=%add | all-reduce | flops 16 | bytes 128
  132.8 11.9 %all-gather = s32[4,4,16]{2,1,0:T(4,128)S(1)} all-gather(s32[1,4,16]{2,1,0:T(4,128)S(1)} %bitcast.126), channel_id=1, replica_groups=mesh['row'=2,'col'=4,'box'=4] {'col'}, dimensions={0}, use_global_device_ids=true | all-gather | bytes 1280 | tf_op jit(solution)/shard_map/all_gather | solution.py:83
  144.8 29.7 %while.10 = (s32[]{:T(128)}, bf16[8,2,128]{2,1,0:T(2,128)(2,1)S(1)}, s32[8,2]{1,0:T(8,128)S(1)}, s32[8,2,16]{2,1,0:T(2,128)S(1)}, f32[16,128]{1,0:T(8,128)S(1)},...) while((s32[]{:T(128)}, ...), condition=%wide.region_3.4_spmd, body=%wide.region_1.3_spmd.sunk | while | flops 140055680 | bytes 3644613 | solution.py:45
  144.9 0.6 gather_fusion.1
  145.7 0.7 gather_fusion
  146.5 0.6 gather_fusion.2
  147.3 1.2 fusion.41
  148.7 0.6 gather_fusion.1
  149.4 0.7 gather_fusion
  150.2 0.6 gather_fusion.2
  151.0 1.2 fusion.41
  152.4 0.6 gather_fusion.1
  153.2 0.7 gather_fusion
  154.7 1.2 fusion.41
  156.1 0.6 gather_fusion.1
  156.9 0.7 gather_fusion
  158.4 1.2 fusion.41
  159.8 0.6 gather_fusion.1
  160.6 0.7 gather_fusion
  162.2 1.2 fusion.41
  163.5 0.6 gather_fusion.1
  164.3 0.7 gather_fusion
  165.9 1.2 fusion.41
  167.2 0.6 gather_fusion.1
  168.0 0.7 gather_fusion
  169.6 1.2 fusion.41
  170.9 0.6 gather_fusion.1
  171.7 0.7 gather_fusion
  173.3 1.2 fusion.41
  174.5 8.6 %all-reduce.1 = bf16[16,128]{1,0:T(8,128)(2,1)S(1)} all-reduce(bf16[16,128]{1,0:T(8,128)(2,1)S(1)} %bitcast.125), channel_id=2, replica_groups=mesh['row'=2,'col'=4,'box'=4] {'col'}, use_global_device_ids=true, to_apply=%region_4.5.clone | all-reduce | flops 2048 | bytes 8192
  183.1 0.6 dynamic-slice_convert_fusion
  (165 shorter events, 8.4 us)
Async XLA Ops:
  7.2 78.4 %copy-start = (s32[81920]{0:T(1024)S(1)}, s32[81920]{0:T(1024)}, u32[]{:S(2)}) copy-start(s32[81920]{0:T(1024)} %param.16) | copy-start | bytes 983044
  7.2 10.8 %copy-start.2 = (s32[8,8,2]{1,2,0:T(2,128)S(1)}, s32[8,8,2]{1,2,0:T(2,128)}, u32[]{:S(2)}) copy-start(s32[8,8,2]{1,2,0:T(2,128)} %param.19) | copy-start | bytes 1540
  7.2 63.0 %all-reduce.4.cloned.1.call-start = ((), (), s32[]{:S(2)}) async-start(), calls=%async_computation.1 | async-start | bytes 131072 | tf_op jit(solution)/shard_map/psum | solution.py:62
  7.2 90.2 %collective-permute-start = (f32[3,4,128]{2,1,0:T(4,128)}, f32[3,4,128]{2,1,0:T(4,128)S(1)}, u32[]{:S(2)}, u32[]{:S(2)}) collective-permute-start(f32[3,4,128]{2,1,0:T(4,128)} %param.18), channel_id=1, source_target_pairs={{0,4},{4,8},{8,12},{12,0},{1,5},{5,9},{9,13},{13,1},{2,6},{6,10},{... | collective-permute-start | bytes 18440 | tf_op jit(solution)/shard_map/ppermute | solution.py:91
  10.3 134.4 %collective-permute-start.2 = (f32[3,4,128]{2,1,0:T(4,128)}, f32[3,4,128]{2,1,0:T(4,128)S(1)}, u32[]{:S(2)}, u32[]{:S(2)}) collective-permute-start(f32[3,4,128]{2,1,0:T(4,128)} %param.18), channel_id=1, source_target_pairs={{0,12},{4,0},{8,4},{12,8},{1,13},{5,1},{9,5},{13,9},{2,14},{6,2},{... | collective-permute-start | bytes 18440 | tf_op jit(solution)/shard_map/ppermute | solution.py:93
  18.9 51.3 %copy-start.4 = (f32[256,256]{1,0:T(8,128)S(1)}, f32[256,256]{1,0:T(8,128)}, u32[]{:S(2)}) copy-start(f32[256,256]{1,0:T(8,128)} %param.14) | copy-start | bytes 786436
  80.4 17.0 %copy-start.3 = (bf16[10240,128]{1,0:T(8,128)(2,1)}, bf16[10240,128]{1,0:T(8,128)(2,1)S(1)}, u32[]{:S(2)}) copy-start(bf16[10240,128]{1,0:T(8,128)(2,1)S(1)} %copy.34) | copy-start | bytes 7864324
  82.0 62.8 %all-to-all-start = ((bf16[8,2,128,128]{3,2,1,0:T(8,128)(2,1)}), bf16[8,2,128,128]{3,2,1,0:T(8,128)(2,1)S(1)}, u32[]{:S(2)}, u32[]{:S(2)}) async-start(bf16[8,2,128,128]{3,2,1,0:T(8,128)(2,1)} %bitcast.116), calls=%async_computation | async-start | bytes 1048576 | tf_op jit(solution)/shard_map/all_to_all | solution.py:80
  97.4 47.3 %collective-permute-start.1 = (f32[3,4,128]{2,1,0:T(4,128)S(1)}, f32[3,4,128]{2,1,0:T(4,128)S(1)}, u32[]{:S(2)}, u32[]{:S(2)}) collective-permute-start(f32[3,4,128]{2,1,0:T(4,128)S(1)} %collective-permute-done), channel_id=1, source_target_pairs={{0,4},{4,8},{8,12},{12,0},{1,5},{5,9},{9,13},{13,1},{2,6},{6,10},{... | collective-permute-start | bytes 18440 | tf_op jit(solution)/shard_map/ppermute | solution.py:91
  99.0 11.5 %copy-start.1 = (f32[81920]{0:T(1024)S(1)}, f32[81920]{0:T(1024)}, u32[]{:S(2)}) copy-start(f32[81920]{0:T(1024)} %param.15) | copy-start | bytes 983044
  110.4 11.8 %copy-start.7 = (u32[32]{0:T(128)S(1)}, u32[32]{0:T(128)}, u32[]{:S(2)}) copy-start(u32[32]{0:T(128)} %constant.133) | copy-start | bytes 388
  110.4 13.2 %copy-start.8 = (s32[4]{0:T(128)S(1)}, s32[4]{0:T(128)}, u32[]{:S(2)}) copy-start(s32[4]{0:T(128)} %param.21) | copy-start | bytes 52
  110.4 22.4 %copy-start.6 = (s32[4,16]{1,0:T(4,128)S(1)}, s32[4,16]{1,0:T(4,128)}, u32[]{:S(2)}) copy-start(s32[4,16]{1,0:T(4,128)} %param.20) | copy-start | bytes 772
  110.5 34.3 %copy-start.5 = (f32[3,4,128]{2,1,0:T(4,128)S(1)}, f32[3,4,128]{2,1,0:T(4,128)}, u32[]{:S(2)}) copy-start(f32[3,4,128]{2,1,0:T(4,128)} %param.18) | copy-start | bytes 18436
Sparse Core Ops, SparseCore 0:
  18.1 52.0 all-reduce.3
